TPU v7x, 256 devices: a whole 4x4x8 slice. The times are simulated.
256 devices in a mesh: row: 8 (over y, x_lo), col: 32 (over x_hi, z, core).
Axes of the slice: x: 4 (x_hi: 2, x_lo: 2; x = x_hi * 2 + x_lo), y: 4, z: 8, core: 2. Of those that a mesh axis runs over, the one named last changes fastest.
Arguments:
- inv_sep: bfloat16 [24576, 24576], P('row', 'col'), may hold values from -6 to 6
- lower_one: bfloat16 [24576, 256], P('col', 'row'), may hold values from -0.0390625 to 0.0390625
- upper_one: bfloat16 [256, 24576], P('col', 'row'), may hold values from -0.0390625 to 0.0390625
- diag_inv_one: float32 [256, 256], replicated, may hold values from -6 to 6
- blocks_one: int32 [160], replicated, may hold values from 0 to 191, as said below
- lower_two: bfloat16 [24576, 256], P('col', 'row'), may hold values from -0.046875 to 0.046875
- upper_two: bfloat16 [256, 24576], P('col', 'row'), may hold values from -0.046875 to 0.046875
- corner_lower: bfloat16 [256, 256], replicated, may hold values from -0.375 to 0.375
- corner_upper: bfloat16 [256, 256], replicated, may hold values from -0.375 to 0.375
- diag_inv_two: float32 [256, 256], replicated, may hold values from -6 to 6
- blocks_two: int32 [128], replicated, may hold values from 0 to 191, as said below
Outputs:
- inv_lower_one: bfloat16 [20480, 256], P(('row', 'col'))
- inv_upper_one: bfloat16 [256, 20480], P('row', 'col')
- inv_diag_one: float32 [256, 256], replicated
- inv_lower_two: bfloat16 [16384, 256], P(('row', 'col'))
- inv_upper_two: bfloat16 [256, 16384], P('row', 'col')
- inv_diag_two: float32 [256, 256], replicated
Inputs may be any that keep to these rules, and one draw needn't show every extreme that they name: `blocks_one`: distinct block indices in increasing order; each aligned run of 6 blocks holds exactly 5 of them; the first and the last block of the separator are listed. `blocks_two`: distinct block indices in increasing order, each of them also in blocks_one; each aligned run of 6 blocks holds exactly 4 of them; the first and the last block of the separator are listed.
All inputs are finite; a program needn't handle non-finite values.
Results may differ from a plain program's by a relative error of at most 0.0039.
Values may be sent and summed in bfloat16 or wider, within the bound.
A program may use at most 64 MiB of HBM per device.

v0:
```python
import jax
import jax.numpy as jnp
from jax import lax
from jax.sharding import PartitionSpec as P

B = 128


def highest(first_mat, second_mat):
    return jnp.dot(
        first_mat.astype(jnp.float32),
        second_mat.astype(jnp.float32),
        precision=lax.Precision.HIGHEST,
    )


def take_rows(matrix, blocks):
    shaped = matrix.reshape(matrix.shape[0] // B, B, matrix.shape[1])
    return jnp.take(shaped, blocks, axis=0).reshape(blocks.shape[0] * B, matrix.shape[1])


def take_cols(matrix, blocks):
    shaped = matrix.reshape(matrix.shape[0], matrix.shape[1] // B, B)
    return jnp.take(shaped, blocks, axis=1).reshape(matrix.shape[0], blocks.shape[0] * B)


def block_rows(blocks):
    return (blocks[:, None] * B + jnp.arange(B, dtype=jnp.int32)[None, :]).reshape(-1)


def places(wanted, listed):
    return jnp.sum((listed[None, :] < wanted[:, None]).astype(jnp.int32), axis=1)


def on_device(
    inv_sep,
    lower_one,
    upper_one,
    diag_inv_one,
    blocks_one,
    lower_two,
    upper_two,
    corner_lower,
    corner_upper,
    diag_inv_two,
    blocks_two,
):
    row_index = lax.axis_index("row")
    col_index = lax.axis_index("col")
    row_count = lax.axis_size("row")
    col_count = lax.axis_size("col")
    rows_here, cols_here = inv_sep.shape
    panel_width = diag_inv_one.shape[0]
    run_blocks = cols_here // B
    pick_one = blocks_one.shape[0] // col_count
    pick_two = blocks_two.shape[0] // col_count
    runs_group = col_count // row_count
    group_one = pick_one * runs_group
    group_two = pick_two * runs_group
    share_one = pick_one * B // row_count
    share_two = pick_two * B // row_count
    upper_rows = panel_width // row_count
    row_one = lax.dynamic_slice_in_dim(blocks_one, row_index * group_one, group_one) - row_index * (
        rows_here // B
    )
    row_two = lax.dynamic_slice_in_dim(blocks_two, row_index * group_two, group_two) - row_index * (
        rows_here // B
    )
    col_one = (
        lax.dynamic_slice_in_dim(blocks_one, col_index * pick_one, pick_one)
        - col_index * run_blocks
    )
    col_two = (
        lax.dynamic_slice_in_dim(blocks_two, col_index * pick_two, pick_two)
        - col_index * run_blocks
    )
    sep_one = take_cols(take_rows(inv_sep, row_one), col_one)
    sep_two = take_cols(take_rows(inv_sep, row_two), col_two)
    lower_spots = block_rows(places(row_two, row_one))
    upper_spots = places(col_two, col_one)
    corner_mine = lax.dynamic_slice_in_dim(corner_upper, row_index * upper_rows, upper_rows, 1)
    lower_p = lax.all_gather(take_rows(lower_one, col_one), "row", axis=1, tiled=True)
    upper_p = lax.all_gather(take_cols(upper_one, row_one), "col", axis=0, tiled=True)
    inv_lower_one = lax.psum_scatter(
        -jnp.dot(sep_one, lower_p, preferred_element_type=jnp.float32),
        "col",
        scatter_dimension=0,
        tiled=True,
    ).astype(jnp.bfloat16)
    inv_upper_one = lax.psum_scatter(
        -jnp.dot(upper_p, sep_one, preferred_element_type=jnp.float32),
        "row",
        scatter_dimension=0,
        tiled=True,
    ).astype(jnp.bfloat16)
    lower_c = lax.all_gather(take_rows(lower_two, col_two), "row", axis=1, tiled=True)
    upper_c = lax.all_gather(take_cols(upper_two, row_two), "col", axis=0, tiled=True)
    own_rows = col_index * share_one + jnp.arange(share_one, dtype=jnp.int32)
    chooser = (lower_spots[:, None] == own_rows[None, :]).astype(jnp.float32)
    carried = jnp.dot(inv_lower_one, corner_lower, preferred_element_type=jnp.float32)
    direct = jnp.dot(sep_two, lower_c, preferred_element_type=jnp.float32)
    shifted_part = jnp.dot(chooser, carried, precision=lax.Precision.HIGHEST)
    inv_lower_two = lax.psum_scatter(
        -(direct + shifted_part), "col", scatter_dimension=0, tiled=True
    ).astype(jnp.bfloat16)
    ancestor_cols = take_cols(inv_upper_one, upper_spots)
    direct = jnp.dot(upper_c, sep_two, preferred_element_type=jnp.float32)
    shifted_part = jnp.dot(corner_mine, ancestor_cols, preferred_element_type=jnp.float32)
    inv_upper_two = lax.psum_scatter(
        -(direct + shifted_part), "row", scatter_dimension=0, tiled=True
    ).astype(jnp.bfloat16)
    upper_slab = lax.dynamic_slice_in_dim(upper_p, col_index * share_one, share_one, 1)
    second_slab = lax.dynamic_slice_in_dim(upper_c, col_index * share_two, share_two, 1)
    first_part = jnp.dot(upper_slab, inv_lower_one, preferred_element_type=jnp.float32)
    cross = jnp.dot(ancestor_cols, lower_c, preferred_element_type=jnp.float32)
    second_part = jnp.dot(second_slab, inv_lower_two, preferred_element_type=jnp.float32) - highest(
        corner_mine, cross
    )
    first_total = lax.psum(first_part, ("row", "col"))
    inv_diag_one = diag_inv_one - first_total
    second_total = lax.psum(second_part, ("row", "col"))
    tail_term = highest(corner_upper, highest(inv_diag_one, corner_lower))
    inv_diag_two = diag_inv_two - (second_total - tail_term)
    return (inv_lower_one, inv_upper_one, inv_diag_one, inv_lower_two, inv_upper_two, inv_diag_two)


def solution(mesh):
    return jax.shard_map(
        on_device,
        mesh=mesh,
        in_specs=(
            P("row", "col"),
            P("col", "row"),
            P("col", "row"),
            P(),
            P(),
            P("col", "row"),
            P("col", "row"),
            P(),
            P(),
            P(),
            P(),
        ),
        out_specs=(
            P(("row", "col"), None),
            P("row", "col"),
            P(),
            P(("row", "col"), None),
            P("row", "col"),
            P(),
        ),
        check_vma=False,
    )
```

profile of v0, /device:TPU:2, one launch (start us, length us, event | category | flops | bytes accessed | tf_op | source)
XLA Modules:
  0.0 767.2 jit_solution(17721407719966944696)
XLA Ops:
  7.2 0.8 compare_and_fusion.3
  8.1 1.4 gather_fusion.3
  9.5 0.6 bitcast_select_fusion.3
  10.2 5.3 gather_fusion
  15.5 9.2 %reshape.206 = bf16[2560,6,128]{2,1,0:T(8,128)(2,1)} reshape(bf16[20,128,768]{2,1,0:T(8,128)(2,1)} %gather_fusion) | data formatting | bytes 7864320 | tf_op jit(solution)/shard_map/jit(_take)/gather | solution.py:19
  24.7 5.2 copy_select_fusion
  30.0 3.3 gather_fusion.1
  33.3 3.4 copy.41
  36.8 0.6 gather_fusion.2
  37.4 29.7 %all_gather.12 = bf16[640,256]{0,1:T(8,128)(2,1)S(1)} all-gather(bf16[640,32]{0,1:T(8,128)(2,1)S(1)} %bitcast_select_fusion.2), channel_id=1, replica_groups=mesh['row'=8,'col'=32] {'row'}, dimensions={1}, use_global_device_ids=true | all-gather | bytes 368640 | tf_op jit(solution)/shard_map/all_gather | solution.py:82
  67.2 2.3 bitcast_select_fusion
  69.5 2.8 convolution_negate_fusion
  72.3 19.8 %all-gather.3.cloned.1.call-done = bf16[256,2560]{1,0:T(8,128)(2,1)} async-done(((bf16[8,2560]{1,0:T(8,128)(2,1)}), bf16[256,2560]{1,0:T(8,128)(2,1)}) %all-gather.3.cloned.1.call-update) | async-done | bytes 1310736 | tf_op jit(solution)/shard_map/all_gather | solution.py:83
  92.1 3.4 convolution_negate_fusion.1
  95.8 0.6 gather_fusion.7
  96.4 0.6 bitcast_select_fusion.6
  97.1 3.1 gather_fusion.4
  100.2 0.2 convert_reduce_fusion
  100.4 4.6 reshape.207
  105.0 2.8 copy_select_fusion.1
  108.1 0.6 gather_fusion.6
  108.6 2.2 gather_fusion.5
  110.8 4.0 copy.46
  114.8 28.8 %all_gather.14 = bf16[512,256]{0,1:T(8,128)(2,1)S(1)} all-gather(bf16[512,32]{0,1:T(8,128)(2,1)S(1)} %bitcast_select_fusion.5), channel_id=1, replica_groups=mesh['row'=8,'col'=32] {'row'}, dimensions={1}, use_global_device_ids=true | all-gather | bytes 294912 | tf_op jit(solution)/shard_map/all_gather | solution.py:96
  143.7 2.1 bitcast_select_fusion.1
  145.8 2.1 fusion.24
  147.9 66.1 %reduce-scatter.5.cloned.1.call-done = f32[80,256]{1,0:T(8,128)} async-done(((f32[2560,256]{1,0:T(8,128)}), f32[80,256]{1,0:T(8,128)}) %reduce-scatter.5.cloned.1.call-update) | async-done | bytes 81936 | tf_op jit(solution)/shard_map/reduce_scatter | solution.py:84
  213.9 0.9 convert_element_type.22
  215.0 3.5 fusion
  218.6 0.2 convert_reduce_fusion.1
  218.9 35.1 %reduce-scatter.7.cloned.1.call-done = f32[32,640]{1,0:T(8,128)} async-done(((f32[256,640]{1,0:T(8,128)}), f32[32,640]{1,0:T(8,128)}) %reduce-scatter.7.cloned.1.call-update) | async-done | bytes 81936 | tf_op jit(solution)/shard_map/reduce_scatter | solution.py:90
  253.9 0.9 copy_bitcast_fusion.2
  254.8 0.6 gather_fusion.8
  255.4 0.3 fusion.12
  255.7 80.1 %all-gather.5.cloned.1.call-done = bf16[256,2048]{1,0:T(8,128)(2,1)} async-done(((bf16[8,2048]{1,0:T(8,128)(2,1)}), bf16[256,2048]{1,0:T(8,128)(2,1)}) %all-gather.5.cloned.1.call-update) | async-done | bytes 1048592 | tf_op jit(solution)/shard_map/all_gather | solution.py:97
  335.8 2.8 fusion.1
  338.9 1.9 fusion.9
  340.7 115.8 %reduce-scatter.9.cloned.1.call-done = f32[64,256]{1,0:T(8,128)} async-done(((f32[2048,256]{1,0:T(8,128)}), f32[64,256]{1,0:T(8,128)}) %reduce-scatter.9.cloned.1.call-update) | async-done | bytes 65552 | tf_op jit(solution)/shard_map/reduce_scatter | solution.py:103
  456.5 0.8 convert_element_type.25
  457.4 1.1 fusion.7
  458.5 1.0 convolution_subtract_fusion
  459.5 0.6 convert_element_type.23
  460.2 35.7 %reduce-scatter.11.cloned.1.call-done = f32[32,512]{1,0:T(8,128)} async-done(((f32[256,512]{1,0:T(8,128)}), f32[32,512]{1,0:T(8,128)}) %reduce-scatter.11.cloned.1.call-update) | async-done | bytes 65552 | tf_op jit(solution)/shard_map/reduce_scatter | solution.py:109
  495.8 1.5 convert_element_type.27
  497.3 259.8 %all-reduce.3.cloned.1.call-done = (f32[256,256]{1,0:T(8,128)}, f32[256,256]{1,0:T(8,128)}) async-done(((f32[256,256]{1,0:T(8,128)}, f32[256,256]{1,0:T(8,128)}), (f32[256,256]{1,0:T(8,128)}, f32[256,256]{1,0:T(8,128)})) %all-reduce.3.cloned.1.call-update) | async-done | bytes 524304 | tf_op jit(solution)/shard_map/psum | solution.py:119
  757.1 1.0 sub.40
  758.1 0.3 fusion.26
  758.4 2.0 fusion.3
  (68 shorter events, 1.6 us)
Async XLA Ops:
  7.2 248.2 %copy-start = (bf16[256,256]{1,0:T(8,128)(2,1)S(1)}, bf16[256,256]{1,0:T(8,128)(2,1)}, u32[]{:S(2)}) copy-start(bf16[256,256]{1,0:T(8,128)(2,1)} %param.19) | copy-start | bytes 393220
  7.2 85.0 %all-gather.3.cloned.1.call-start = ((), (), s32[]{:S(2)}) async-start(), calls=%async_computation.5 | async-start | bytes 1351680 | tf_op jit(solution)/shard_map/all_gather | solution.py:83
  10.1 203.8 %reduce-scatter.5.cloned.1.call-start = ((), (), s32[]{:S(2)}) async-start(), calls=%async_computation.4 | async-start | bytes 2703360 | tf_op jit(solution)/shard_map/reduce_scatter | solution.py:84
  24.7 5.2 copy-start.12
  33.3 3.4 copy-start.8
  72.3 23.4 %copy-start.11 = (s32[128]{0:T(128)S(1)}, s32[128]{0:T(128)}, u32[]{:S(2)}) copy-start(s32[128]{0:T(128)} %param.21) | copy-start | bytes 1540
  72.3 23.5 %copy-start.10 = (bf16[8,3072]{1,0:T(8,128)(2,1)S(1)}, bf16[8,3072]{1,0:T(8,128)(2,1)}, u32[]{:S(2)}) copy-start(bf16[8,3072]{1,0:T(8,128)(2,1)} %param.17) | copy-start | bytes 147460
  72.3 181.6 %reduce-scatter.7.cloned.1.call-start = ((), (), s32[]{:S(2)}) async-start(), calls=%async_computation.6 | async-start | bytes 737280 | tf_op jit(solution)/shard_map/reduce_scatter | solution.py:90
  95.6 240.2 %all-gather.5.cloned.1.call-start = ((), (), s32[]{:S(2)}) async-start(), calls=%async_computation.8 | async-start | bytes 1081344 | tf_op jit(solution)/shard_map/all_gather | solution.py:97
  97.1 359.5 %reduce-scatter.9.cloned.1.call-start = ((), (), s32[]{:S(2)}) async-start(), calls=%async_computation.7 | async-start | bytes 2162688 | tf_op jit(solution)/shard_map/reduce_scatter | solution.py:103
  105.0 3.0 copy-start.9
  145.8 69.1 %copy-start.2 = (bf16[256,256]{1,0:T(8,128)(2,1)S(1)}, bf16[256,256]{1,0:T(8,128)(2,1)}, u32[]{:S(2)}) copy-start(bf16[256,256]{1,0:T(8,128)(2,1)} %param.18) | copy-start | bytes 393220
  214.8 124.0 %copy-start.3 = (bf16[80,256]{1,0:T(8,128)(2,1)}, bf16[80,256]{1,0:T(8,128)(2,1)S(1)}, u32[]{:S(2)}) copy-start(bf16[80,256]{1,0:T(8,128)(2,1)S(1)} %convert_element_type.22) | copy-start | bytes 122884
  218.5 277.3 %reduce-scatter.11.cloned.1.call-start = ((), (), s32[]{:S(2)}) async-start(), calls=%async_computation.9 | async-start | bytes 589824 | tf_op jit(solution)/shard_map/reduce_scatter | solution.py:109
  255.7 203.9 %copy-start.4 = (f32[32,640]{1,0:T(8,128)S(1)}, f32[32,640]{1,0:T(8,128)}, u32[]{:S(2)}) copy-start(f32[32,640]{1,0:T(8,128)} %reduce-scatter.7.cloned.1.call-done) | copy-start | bytes 245764
  338.6 418.5 %copy-start.5 = (f32[256,256]{1,0:T(8,128)S(1)}, f32[256,256]{1,0:T(8,128)}, u32[]{:S(2)}) copy-start(f32[256,256]{1,0:T(8,128)} %param.14) | copy-start | bytes 786436
  338.6 419.8 %copy-start.6 = (f32[256,256]{1,0:T(8,128)S(1)}, f32[256,256]{1,0:T(8,128)}, u32[]{:S(2)}) copy-start(f32[256,256]{1,0:T(8,128)} %param.20) | copy-start | bytes 786436
  338.6 418.5 %all-reduce.3.cloned.1.call-start = ((), (), s32[]{:S(2)}) async-start(), calls=%async_computation.10 | async-start | bytes 1048576 | tf_op jit(solution)/shard_map/psum | solution.py:119
  457.4 303.0 %copy-start.7 = (bf16[64,256]{1,0:T(8,128)(2,1)}, bf16[64,256]{1,0:T(8,128)(2,1)S(1)}, u32[]{:S(2)}) copy-start(bf16[64,256]{1,0:T(8,128)(2,1)S(1)} %convert_element_type.25) | copy-start | bytes 98308
  758.1 2.3 copy-start.1
Sparse Core Ops, SparseCore 0:
  11.4 80.7 all-gather.2
  96.3 117.6 reduce-scatter.4
  216.6 37.2 reduce-scatter.6
  257.5 78.2 all-gather.4
  340.3 116.1 reduce-scatter.8
  458.9 36.8 reduce-scatter.10
  502.9 254.1 all-reduce.2
where the time goes:
time: 768 us; the launch traced here: 767 us
  waiting for transfers between devices  612 us (80%)
  blocking collectives  58.5 us (8%)
  local copies, waits for them, and re-layouts  39.2 us (5%)
  matrix products  21.4 us (3%)
  other arithmetic  20.9 us (3%)
  between operations  14.4 us (2%)
    psum x1, waiting for transfers between devices, on_device(): first_total = lax.psum(first_part, ('row', 'col'))  260 us
    reduce_scatter x1, waiting for transfers between devices, on_device(): lax.psum_scatter(-(direct + shifted_part), 'col', scatter_dimension=0, ti...  116 us
    all_gather x1, waiting for transfers between devices, on_device(): lax.all_gather(take_cols(upper_two, row_two), 'col', axis=0, tiled=True)  80.1 us
    reduce_scatter x1, waiting for transfers between devices, on_device(): lax.psum_scatter(-jnp.dot(sep_one, lower_p, preferred_element_type=jnp.fl...  66.1 us
    reduce_scatter x1, waiting for transfers between devices, on_device(): lax.psum_scatter(-(direct + shifted_part), 'row', scatter_dimension=0, ti...  35.7 us
    reduce_scatter x1, waiting for transfers between devices, on_device(): lax.psum_scatter(-jnp.dot(upper_p, sep_one, preferred_element_type=jnp.fl...  35.1 us
    all_gather x1, blocking collectives, on_device(): lax.all_gather(take_rows(lower_one, col_one), 'row', axis=1, tiled=True)  29.7 us
    all_gather x1, blocking collectives, on_device(): lax.all_gather(take_rows(lower_two, col_two), 'row', axis=1, tiled=True)  28.8 us
  transfers between devices with their start and end apart: 7, of which 7 were waited for; matrix products, arithmetic and copies ran while one was open for 10% of the time, Pallas kernels for 0%

commit v1 on v0

--- a/solution.py
+++ b/solution.py
@@ -116,7 +116,7 @@
     second_part = jnp.dot(second_slab, inv_lower_two, preferred_element_type=jnp.float32) - highest(
         corner_mine, cross
     )
-    first_total = lax.psum(first_part, ("row", "col"))
+    first_total = lax.psum(lax.psum(first_part, "row"), "col")
     inv_diag_one = diag_inv_one - first_total
     second_total = lax.psum(second_part, ("row", "col"))
     tail_term = highest(corner_upper, highest(inv_diag_one, corner_lower))

time: 768 us -> 1170 us (1.52)
  waiting for transfers between devices: 612 us -> 1010 us
    psum x1 -> x3, waiting for transfers between devices: 260 us -> 537 us  [the longest x2 280 us: on_device(): first_total = lax.psum(lax.psum(first_part, 'row'), 'col')]
    all_gather x1, waiting for transfers between devices: 19.8 us -> 79.1 us  [on_device(): lax.all_gather(take_cols(upper_one, row_one), 'col', axis=0, tiled=True)]
    reduce_scatter x1, waiting for transfers between devices: 66.1 us -> 121 us  [on_device(): lax.psum_scatter(-jnp.dot(sep_one, lower_p, preferred_element_type=jnp.fl...]
  transfers between devices with their start and end apart: 7 -> 9, of which waited for: 7 -> 9; matrix products, arithmetic and copies ran while one was open for 10% -> 4% of each run, Pallas kernels for 0% -> 0%
where the time goes in v1:
time: 1170 us
  waiting for transfers between devices  1010 us (86%)
  blocking collectives  58.3 us (5%)
  local copies, waits for them, and re-layouts  38.4 us (3%)
  matrix products  21.3 us (2%)
  other arithmetic  20.7 us (2%)
  between operations  14.1 us (1%)
    psum x2, waiting for transfers between devices, on_device(): first_total = lax.psum(lax.psum(first_part, 'row'), 'col')  280 us
    psum x1, waiting for transfers between devices, on_device(): second_total = lax.psum(second_part, ('row', 'col'))  257 us
    reduce_scatter x1, waiting for transfers between devices, on_device(): lax.psum_scatter(-jnp.dot(sep_one, lower_p, preferred_element_type=jnp.fl...  121 us
    reduce_scatter x1, waiting for transfers between devices, on_device(): lax.psum_scatter(-(direct + shifted_part), 'col', scatter_dimension=0, ti...  121 us
    all_gather x1, waiting for transfers between devices, on_device(): lax.all_gather(take_cols(upper_two, row_two), 'col', axis=0, tiled=True)  79.7 us
    all_gather x1, waiting for transfers between devices, on_device(): lax.all_gather(take_cols(upper_one, row_one), 'col', axis=0, tiled=True)  79.1 us
    reduce_scatter x1, waiting for transfers between devices, on_device(): lax.psum_scatter(-jnp.dot(upper_p, sep_one, preferred_element_type=jnp.fl...  38.4 us
    reduce_scatter x1, waiting for transfers between devices, on_device(): lax.psum_scatter(-(direct + shifted_part), 'row', scatter_dimension=0, ti...  36 us
  transfers between devices with their start and end apart: 9, of which 9 were waited for; matrix products, arithmetic and copies ran while one was open for 4% of the time, Pallas kernels for 0%

profile of v1, /device:TPU:2, one launch (start us, length us, event | category | flops | bytes accessed | tf_op | source)
XLA Modules:
  0.0 1166.6 jit_solution(13566333004282500684)
XLA Ops:
  7.2 0.8 compare_and_fusion.3
  8.0 5.3 gather_fusion
  13.3 9.2 reshape.206
  22.7 5.3 copy_select_fusion
  28.0 3.3 gather_fusion.1
  31.3 3.4 copy.41
  34.8 0.6 gather_fusion.2
  35.4 2.3 bitcast_select_fusion
  37.7 29.5 %all_gather.12 = bf16[640,256]{0,1:T(8,128)(2,1)S(1)} all-gather(bf16[640,32]{0,1:T(8,128)(2,1)S(1)} %bitcast_select_fusion.2), channel_id=1, replica_groups=mesh['row'=8,'col'=32] {'row'}, dimensions={1}, use_global_device_ids=true | all-gather | bytes 368640 | tf_op jit(solution)/shard_map/all_gather | solution.py:82
  67.2 2.7 convolution_negate_fusion
  70.0 0.6 gather_fusion.3
  70.6 0.6 bitcast_select_fusion.3
  71.3 121.5 %reduce-scatter.5.cloned.1.call-done = f32[80,256]{1,0:T(8,128)} async-done(((f32[2560,256]{1,0:T(8,128)}), f32[80,256]{1,0:T(8,128)}) %reduce-scatter.5.cloned.1.call-update) | async-done | bytes 81936 | tf_op jit(solution)/shard_map/reduce_scatter | solution.py:84
  192.7 0.9 convert_element_type.22
  193.6 79.1 %all-gather.3.cloned.1.call-done = bf16[256,2560]{1,0:T(8,128)(2,1)} async-done(((bf16[8,2560]{1,0:T(8,128)(2,1)}), bf16[256,2560]{1,0:T(8,128)(2,1)}) %all-gather.3.cloned.1.call-update) | async-done | bytes 1310736 | tf_op jit(solution)/shard_map/all_gather | solution.py:83
  272.7 1.8 fusion.9
  274.6 3.4 convolution_negate_fusion.1
  278.2 0.6 gather_fusion.7
  278.9 0.6 bitcast_select_fusion.6
  279.6 3.1 gather_fusion.4
  282.7 4.7 reshape.207
  287.4 2.8 copy_select_fusion.1
  290.3 2.2 gather_fusion.5
  292.5 4.0 copy.46
  296.5 0.6 gather_fusion.6
  297.2 28.8 %all_gather.14 = bf16[512,256]{0,1:T(8,128)(2,1)S(1)} all-gather(bf16[512,32]{0,1:T(8,128)(2,1)S(1)} %bitcast_select_fusion.5), channel_id=1, replica_groups=mesh['row'=8,'col'=32] {'row'}, dimensions={1}, use_global_device_ids=true | all-gather | bytes 294912 | tf_op jit(solution)/shard_map/all_gather | solution.py:96
  326.1 1.8 bitcast_select_fusion.1
  328.0 2.1 fusion.24
  330.2 20.3 %all-reduce.4.cloned.1.call-done = f32[256,256]{1,0:T(8,128)} async-done(((f32[256,256]{1,0:T(8,128)}), f32[256,256]{1,0:T(8,128)}) %all-reduce.4.cloned.1.call-update) | async-done | bytes 262160 | tf_op jit(solution)/shard_map/psum | solution.py:119
  350.6 3.5 fusion
  354.5 38.4 %reduce-scatter.7.cloned.1.call-done = f32[32,640]{1,0:T(8,128)} async-done(((f32[256,640]{1,0:T(8,128)}), f32[32,640]{1,0:T(8,128)}) %reduce-scatter.7.cloned.1.call-update) | async-done | bytes 81936 | tf_op jit(solution)/shard_map/reduce_scatter | solution.py:90
  392.9 1.0 copy_bitcast_fusion.2
  393.9 0.6 gather_fusion.8
  394.4 0.3 fusion.12
  394.7 79.7 %all-gather.5.cloned.1.call-done = bf16[256,2048]{1,0:T(8,128)(2,1)} async-done(((bf16[8,2048]{1,0:T(8,128)(2,1)}), bf16[256,2048]{1,0:T(8,128)(2,1)}) %all-gather.5.cloned.1.call-update) | async-done | bytes 1048592 | tf_op jit(solution)/shard_map/all_gather | solution.py:97
  474.4 2.8 fusion.1
  477.3 0.6 convert_element_type.23
  478.1 259.5 %all-reduce.6.cloned.1.call-done = f32[256,256]{1,0:T(8,128)} async-done(((f32[256,256]{1,0:T(8,128)}), f32[256,256]{1,0:T(8,128)}) %all-reduce.6.cloned.1.call-update) | async-done | bytes 262160 | tf_op jit(solution)/shard_map/psum | solution.py:119
  737.6 1.0 sub.40
  738.6 121.4 %reduce-scatter.9.cloned.1.call-done = f32[64,256]{1,0:T(8,128)} async-done(((f32[2048,256]{1,0:T(8,128)}), f32[64,256]{1,0:T(8,128)}) %reduce-scatter.9.cloned.1.call-update) | async-done | bytes 65552 | tf_op jit(solution)/shard_map/reduce_scatter | solution.py:103
  860.1 0.8 convert_element_type.25
  860.9 1.1 fusion.7
  862.0 1.0 convolution_subtract_fusion
  863.1 0.3 fusion.26
  863.3 36.0 %reduce-scatter.11.cloned.1.call-done = f32[32,512]{1,0:T(8,128)} async-done(((f32[256,512]{1,0:T(8,128)}), f32[32,512]{1,0:T(8,128)}) %reduce-scatter.11.cloned.1.call-update) | async-done | bytes 65552 | tf_op jit(solution)/shard_map/reduce_scatter | solution.py:109
  899.4 1.5 convert_element_type.27
  900.8 257.2 %all-reduce.8.cloned.1.call-done = f32[256,256]{1,0:T(8,128)} async-done(((f32[256,256]{1,0:T(8,128)}), f32[256,256]{1,0:T(8,128)}) %all-reduce.8.cloned.1.call-update) | async-done | bytes 262160 | tf_op jit(solution)/shard_map/psum | solution.py:121
  1158.1 2.0 fusion.3
  (76 shorter events, 2.1 us)
Async XLA Ops:
  7.2 387.3 %copy-start = (bf16[256,256]{1,0:T(8,128)(2,1)S(1)}, bf16[256,256]{1,0:T(8,128)(2,1)}, u32[]{:S(2)}) copy-start(bf16[256,256]{1,0:T(8,128)(2,1)} %param.19) | copy-start | bytes 393220
  7.2 185.5 %reduce-scatter.5.cloned.1.call-start = ((), (), s32[]{:S(2)}) async-start(), calls=%async_computation.4 | async-start | bytes 2703360 | tf_op jit(solution)/shard_map/reduce_scatter | solution.py:84
  13.3 9.3 copy-start.13
  31.3 3.5 copy-start.8
  67.2 2.8 copy-start.9
  69.9 202.8 %all-gather.3.cloned.1.call-start = ((), (), s32[]{:S(2)}) async-start(), calls=%async_computation.5 | async-start | bytes 1351680 | tf_op jit(solution)/shard_map/all_gather | solution.py:83
  71.2 279.3 %all-reduce.4.cloned.1.call-start = ((), (), s32[]{:S(2)}) async-start(), calls=%async_computation.7 | async-start | bytes 524288 | tf_op jit(solution)/shard_map/psum | solution.py:119
  193.6 136.5 %copy-start.3 = (bf16[80,256]{1,0:T(8,128)(2,1)}, bf16[80,256]{1,0:T(8,128)(2,1)S(1)}, u32[]{:S(2)}) copy-start(bf16[80,256]{1,0:T(8,128)(2,1)S(1)} %convert_element_type.22) | copy-start | bytes 122884
  274.6 3.6 copy-start.12
  274.6 3.7 copy-start.11
  274.6 118.3 %reduce-scatter.7.cloned.1.call-start = ((), (), s32[]{:S(2)}) async-start(), calls=%async_computation.6 | async-start | bytes 737280 | tf_op jit(solution)/shard_map/reduce_scatter | solution.py:90
  278.1 196.4 %all-gather.5.cloned.1.call-start = ((), (), s32[]{:S(2)}) async-start(), calls=%async_computation.10 | async-start | bytes 1081344 | tf_op jit(solution)/shard_map/all_gather | solution.py:97
  279.5 458.1 %all-reduce.6.cloned.1.call-start = ((), (), s32[]{:S(2)}) async-start(), calls=%async_computation.8 | async-start | bytes 524288 | tf_op jit(solution)/shard_map/psum | solution.py:119
  287.3 2.9 copy-start.10
  328.0 2.1 copy-start.2
  350.6 509.5 %reduce-scatter.9.cloned.1.call-start = ((), (), s32[]{:S(2)}) async-start(), calls=%async_computation.9 | async-start | bytes 2162688 | tf_op jit(solution)/shard_map/reduce_scatter | solution.py:103
  354.1 383.5 %copy-start.5 = (f32[256,256]{1,0:T(8,128)S(1)}, f32[256,256]{1,0:T(8,128)}, u32[]{:S(2)}) copy-start(f32[256,256]{1,0:T(8,128)} %param.14) | copy-start | bytes 786436
  354.2 545.2 %reduce-scatter.11.cloned.1.call-start = ((), (), s32[]{:S(2)}) async-start(), calls=%async_computation.11 | async-start | bytes 589824 | tf_op jit(solution)/shard_map/reduce_scatter | solution.py:109
  392.9 84.4 %copy-start.4 = (f32[32,640]{1,0:T(8,128)S(1)}, f32[32,640]{1,0:T(8,128)}, u32[]{:S(2)}) copy-start(f32[32,640]{1,0:T(8,128)} %reduce-scatter.7.cloned.1.call-done) | copy-start | bytes 245764
  477.2 680.8 %copy-start.6 = (f32[256,256]{1,0:T(8,128)S(1)}, f32[256,256]{1,0:T(8,128)}, u32[]{:S(2)}) copy-start(f32[256,256]{1,0:T(8,128)} %param.20) | copy-start | bytes 786436
  477.2 680.8 %all-reduce.8.cloned.1.call-start = ((), (), s32[]{:S(2)}) async-start(), calls=%async_computation.12 | async-start | bytes 524288 | tf_op jit(solution)/shard_map/psum | solution.py:121
  738.6 421.4 %copy-start.1 = (f32[256,256]{1,0:T(8,128)}, f32[256,256]{1,0:T(8,128)S(1)}, u32[]{:S(2)}) copy-start(f32[256,256]{1,0:T(8,128)S(1)} %sub.40) | copy-start | bytes 786436
  860.9 299.1 %copy-start.7 = (bf16[64,256]{1,0:T(8,128)(2,1)}, bf16[64,256]{1,0:T(8,128)(2,1)S(1)}, u32[]{:S(2)}) copy-start(bf16[64,256]{1,0:T(8,128)(2,1)S(1)} %convert_element_type.25) | copy-start | bytes 98308
Sparse Core Ops, SparseCore 0:
  70.0 122.6 reduce-scatter.4
  196.5 76.1 all-gather.2
  276.1 74.4 all-reduce.3
  352.9 39.9 reduce-scatter.6
  396.1 78.2 all-gather.4
  476.9 260.6 all-reduce.5
  742.3 117.6 reduce-scatter.8
  862.6 36.7 reduce-scatter.10
  906.3 251.7 all-reduce.7
